TPU v7x, 32 devices: a whole 2x2x4 slice. The times are simulated.
32 devices in a mesh: level: 8 (over z, y), bal: 4 (over x, core).
Axes of the slice: x: 2, y: 2, z: 4, core: 2. Of those that a mesh axis runs over, the one named last changes fastest.
Arguments:
- patches: float32 [640, 5, 4096], P(('level', 'bal')), may hold values from -6 to 6
- patch_ids: int32 [640], P(('level', 'bal')), may hold values from 0 to 639, each once
- live: int32 [32], P(('level', 'bal')), may hold values from 4 to 12, as said below
- counts: int32 [2, 32], P(None, ('level', 'bal')), may hold values from 0 to 4, as said below
- parent_of: int32 [640], replicated, may hold values from 0 to 15
Outputs:
- new_patches: float32 [640, 5, 4096], P(('level', 'bal'))
- new_ids: int32 [640], P(('level', 'bal'))
- coarse: float32 [16, 5, 512], P('level')
Inputs may be any that keep to these rules, and one draw needn't show every extreme that they name: In every level group one device holds exactly 12 live patches. counts[r, d] never exceeds the live patches of device d at the start of round r; in every round and level group some device sends exactly 4.
All inputs are finite; a program needn't handle non-finite values.
Results may differ from a plain program's by a relative error of at most 0.0003.
Values sent between devices are 32-bit elements; how exact they have to be, the bound alone decides.
A program may use at most 64 MiB of HBM per device.

v0:
```python
import jax
import jax.numpy as jnp
from jax import lax
from jax.sharding import PartitionSpec as P

EDGE = 16
VARS = 5
SEND_MOST = 4
PAR_DEV = 2


def from_partner(array, axis, stride):
    return lax.ppermute(array, axis, [(i, i ^ 1 << stride) for i in range(lax.axis_size(axis))])


def restrict(fine_rows):
    leading = fine_rows.shape[:-1]
    half_edge = EDGE // 2
    blocks = fine_rows.reshape(leading + (half_edge, 2, half_edge, 2, half_edge, 2))
    return jnp.mean(blocks, axis=(-5, -3, -1)).reshape(
        leading + (half_edge * half_edge * half_edge,)
    )


def take_top(fine_rows, fine_ids, held_count, sent_count):
    capacity = fine_rows.shape[0]
    lane_index = jnp.arange(SEND_MOST, dtype=jnp.int32)
    pick_index = jnp.clip(held_count - sent_count + lane_index, 0, capacity - 1)
    is_valid = lane_index < sent_count
    return (
        jnp.where(is_valid[:, None, None], fine_rows[pick_index], 0.0),
        jnp.where(is_valid, fine_ids[pick_index], -1),
    )


def place_rows(fine_rows, fine_ids, kept_count, in_rows, in_ids):
    capacity = fine_rows.shape[0]
    slot_index = jnp.arange(capacity, dtype=jnp.int32)
    offset = slot_index - kept_count
    is_hit = (offset >= 0) & (offset < SEND_MOST)
    place_index = jnp.clip(offset, 0, SEND_MOST - 1)
    is_kept = slot_index < kept_count
    new_rows = jnp.where(
        is_kept[:, None, None],
        fine_rows,
        jnp.where(is_hit[:, None, None], in_rows[place_index], 0.0),
    )
    new_ids = jnp.where(is_kept, fine_ids, jnp.where(is_hit, in_ids[place_index], -1))
    return (new_rows, new_ids)


def pairwise_move(fine_rows, fine_ids, held_count, counts, rounds):
    for turn_index in range(rounds):
        sent_count = counts[turn_index, 0]
        out_rows, out_ids = take_top(fine_rows, fine_ids, held_count, sent_count)
        in_rows, in_marks = from_partner((out_rows, out_ids.astype(jnp.float32)), "bal", turn_index)
        in_ids = in_marks.astype(jnp.int32)
        kept_count = held_count - sent_count
        fine_rows, fine_ids = place_rows(fine_rows, fine_ids, kept_count, in_rows, in_ids)
        held_count = kept_count + jnp.sum((in_ids >= 0).astype(jnp.int32))
    return (fine_rows, fine_ids)


def parent_sums(fine_rows, fine_ids, parent_of):
    capacity = fine_rows.shape[0]
    reduced = restrict(fine_rows).reshape(capacity, -1)
    parent = jnp.where(fine_ids >= 0, parent_of[jnp.clip(fine_ids, 0, parent_of.shape[0] - 1)], -1)
    wanted = jnp.arange(lax.axis_size("level") * PAR_DEV, dtype=jnp.int32)
    one_hot = (wanted[:, None] == parent[None, :]).astype(jnp.float32)
    level_sums = lax.psum_scatter(
        jnp.dot(one_hot, reduced, precision=lax.Precision.HIGHEST),
        "level",
        scatter_dimension=0,
        tiled=True,
    )
    group_sums = lax.psum(level_sums, "bal")
    return group_sums.reshape(PAR_DEV, VARS, -1)


def per_device(patches, patch_ids, live, counts, parent_of):
    capacity = patches.shape[0]
    group = lax.axis_size("bal")
    rounds = group.bit_length() - 1
    slot_index = jnp.arange(capacity, dtype=jnp.int32)
    held_count = live[0]
    is_kept = slot_index < held_count
    fine_rows = jnp.where(is_kept[:, None, None], patches, 0.0)
    fine_ids = jnp.where(is_kept, patch_ids, -1)
    coarse = parent_sums(fine_rows, fine_ids, parent_of)
    fine_rows, fine_ids = pairwise_move(fine_rows, fine_ids, held_count, counts, rounds)
    return (fine_rows, fine_ids, coarse)


def solution(mesh):
    return jax.shard_map(
        per_device,
        mesh=mesh,
        in_specs=(
            P(("level", "bal"), None, None),
            P(("level", "bal")),
            P(("level", "bal")),
            P(None, ("level", "bal")),
            P(),
        ),
        out_specs=(P(("level", "bal"), None, None), P(("level", "bal")), P("level", None, None)),
        check_vma=False,
    )
```

profile of v0, /device:TPU:0, one launch (start us, length us, event | category | flops | bytes accessed | tf_op | source)
XLA Modules:
  0.0 143.0 jit_solution(11142344460428278387)
XLA Ops:
  7.2 1.3 fusion.13
  10.4 2.7 %copy_select_fusion = f32[20,5,4096]{2,1,0:T(8,128)S(1)} fusion(f32[20,5,4096]{2,0,1:T(8,128)} %param.5, pred[20]{0:T(512)(128)(4,1)S(1)} %iota_compare_fusion.4), kind=kLoop, calls=%fused_computation.7 | loop fusion | flops 409600 | bytes 3276820 | tf_op jit(solution)/shard_map/jit(_where)/select_n | solution.py:87
  13.7 0.9 broadcast_select_fusion.1
  16.4 6.2 %copy.14 = f32[20,5,4096]{0,2,1:T(8,128)} copy(f32[20,5,4096]{2,1,0:T(8,128)S(1)} %copy_select_fusion) | data formatting | bytes 3276800 | tf_op jit(solution)/shard_map/jit(_where)/select_n | solution.py:87
  22.6 0.6 iota_compare_fusion.2
  23.3 10.6 %reduce_sum.19 = f32[20,5,8,8,8]{0,4,3,2,1:T(8,128)S(1)} reduce(f32[20,5,8,2,8,2,8,2]{0,7,6,5,4,3,2,1:T(2,128)} %bitcast.30, f32[]{:T(128)} %constant.3.clone.1), dimensions={3,5,7}, to_apply=%region_1.2 | reduce | flops 358400 | bytes 1843204 | tf_op jit(solution)/shard_map/reduce_sum | solution.py:20
  34.1 0.7 gather_fusion.6
  38.0 0.7 fusion.12
  38.7 2.5 %compare_select_fusion.11 = (s32[20]{0:T(128)S(1)}, s32[20]{0:T(128)S(1)}) fusion(s32[20]{0:T(128)S(1)} %gather_fusion.6, s32[20]{0:T(128)S(1)} %get-tuple-element.10, s32[]{:T(128)} %bitcast.10, s32[]{:T(128)} %bitcast.9, s32[]{:T(128)} %bitcast.8, s32[]{:T(128)} %bitcast.7, s32[]{:T(128)S(6)} %sub.42), kind=kLoop, calls=%fused_computation.32 | loop fusion | flops 400 | bytes 340 | tf_op jit(solution)/shard_map/jit(_where)/select_n | solution.py:67
  41.8 0.7 select_convert_fusion
  42.5 3.0 %collective-permute-start.3 = (f32[4]{0:T(128)S(1)}, f32[4]{0:T(128)S(1)}, u32[]{:S(2)}, u32[]{:S(2)}) collective-permute-start(f32[4]{0:T(128)S(1)} %select_convert_fusion), channel_id=1, source_target_pairs={{0,2},{1,3},{2,0},{3,1},{4,6},{5,7},{6,4},{7,5},{8,10},{9,11},{10,... | collective-permute-start | bytes 56 | tf_op jit(solution)/shard_map/ppermute | solution.py:13
  45.5 1.4 fusion
  47.0 0.7 fusion.11
  47.7 3.0 %fusion.5 = s32[20]{0:T(128)} fusion(s32[20]{0:T(128)S(1)} %get-tuple-element.12, s32[]{:T(128)} %bitcast.11, s32[]{:T(128)} %bitcast.12, s32[]{:T(128)} %bitcast.13, s32[]{:T(128)} %bitcast.14, s32[]{:T(128)S(6)} %sub.43), kind=kLoop, calls=%fused_computation.39 | loop fusion | flops 360 | bytes 180 | tf_op jit(solution)/shard_map/jit(_where)/select_n | solution.py:48
  50.7 2.2 %gather_fusion.2 = f32[20,5,4096]{2,1,0:T(8,128)} fusion(f32[4,5,4096]{2,1,0:T(8,128)S(1)} %collective-permute-done.1, s32[1024]{0:T(1024)S(1)} %pad_clamp_fusion.3), kind=kCustom, calls=%fused_computation.2 | custom fusion | bytes 3276880 | tf_op jit(solution)/shard_map/gather | solution.py:46
  52.9 3.8 %select_select_fusion.1 = f32[20,5,4096]{2,1,0:T(8,128)S(1)} fusion(f32[20,5,4096]{2,1,0:T(8,128)} %gather_fusion.2, pred[20]{0:T(512)(128)(4,1)S(1)} %get-tuple-element.23, pred[20]{0:T(512)(128)(4,1)S(1)} %get-tuple-element.24, f32[20,5,4096]{2,0,1:T(8,128)} %param.5, pred[20]{0:T(512)(128)(4,1)S(1)} %iota_compare_fusion.4), kind=kLoop, calls=%fused_computation.9 | loop fusion | flops 1228800 | bytes 4915260 | tf_op jit(solution)/shard_map/jit(_where)/select_n | solution.py:43
  57.3 0.9 broadcast_select_fusion
  58.2 2.0 %collective-permute-start.2 = (f32[4,5,4096]{2,1,0:T(8,128)}, f32[4,5,4096]{2,1,0:T(8,128)S(1)}, u32[]{:S(2)}, u32[]{:S(2)}) collective-permute-start(f32[4,5,4096]{2,1,0:T(8,128)} %broadcast_select_fusion), channel_id=1, source_target_pairs={{0,2},{1,3},{2,0},{3,1},{4,6},{5,7},{6,4},{7,5},{8,10},{9,11},{10,... | collective-permute-start | bytes 983048 | tf_op jit(solution)/shard_map/ppermute | solution.py:13
  60.3 57.1 %all-reduce.3.cloned.1.call-done = f32[16,2560]{1,0:T(8,128)} async-done(((f32[16,2560]{1,0:T(8,128)}), f32[16,2560]{1,0:T(8,128)}) %all-reduce.3.cloned.1.call-update) | async-done | bytes 163856
  117.4 0.9 constant_dynamic-slice_fusion
  118.3 10.3 %psum.7 = f32[2,5,512]{2,1,0:T(8,128)S(1)} all-reduce(f32[2,5,512]{2,1,0:T(8,128)S(1)} %reshape.127), channel_id=1, replica_groups=mesh['level'=8,'bal'=4] {'bal'}, use_global_device_ids=true, to_apply=%region_3.4 | all-reduce | flops 5120 | bytes 40960 | tf_op jit(solution)/shard_map/psum | solution.py:76
  129.2 2.2 %gather_fusion.4 = f32[20,5,4096]{2,1,0:T(8,128)} fusion(f32[4,5,4096]{2,1,0:T(8,128)S(1)} %collective-permute-done.2, s32[1024]{0:T(1024)S(1)} %pad_clamp_fusion.1), kind=kCustom, calls=%fused_computation.4 | custom fusion | bytes 3276880 | tf_op jit(solution)/shard_map/gather | solution.py:46
  131.5 2.4 %select_select_fusion = f32[20,5,4096]{2,1,0:T(8,128)S(1)} fusion(f32[20,5,4096]{2,1,0:T(8,128)S(1)} %select_select_fusion.1, f32[20,5,4096]{2,1,0:T(8,128)} %gather_fusion.4, pred[20]{0:T(512)(128)(4,1)S(1)} %get-tuple-element.25, pred[20]{0:T(512)(128)(4,1)S(1)} %get-tuple-element.26), kind=kLoop, calls=%fused_computation.8 | loop fusion | flops 819200 | bytes 4915240 | tf_op jit(solution)/shard_map/jit(_where)/select_n | solution.py:43
  133.9 2.2 %copy.15 = f32[20,5,4096]{2,0,1:T(8,128)} copy(f32[20,5,4096]{2,1,0:T(8,128)S(1)} %select_select_fusion) | data formatting | bytes 3276800
  (40 shorter events, 6.4 us)
Async XLA Ops:
  7.2 26.9 %copy-start = (s32[640]{0:T(1024)S(1)}, s32[640]{0:T(1024)}, u32[]{:S(2)}) copy-start(s32[640]{0:T(1024)} %param.9) | copy-start | bytes 7684
  7.2 110.2 %all-reduce.3.cloned.1.call-start = ((), (), s32[]{:S(2)}) async-start(), calls=%async_computation | async-start | bytes 327680
  10.4 4.7 %copy-start.1 = (s32[20]{0:T(128)S(1)}, s32[20]{0:T(128)}, u32[]{:S(2)}) copy-start(s32[20]{0:T(128)} %param.6) | copy-start | bytes 244
  14.6 36.1 %collective-permute-start.1 = (f32[4,5,4096]{2,1,0:T(8,128)}, f32[4,5,4096]{2,1,0:T(8,128)S(1)}, u32[]{:S(2)}, u32[]{:S(2)}) collective-permute-start(f32[4,5,4096]{2,1,0:T(8,128)} %broadcast_select_fusion.1), channel_id=1, source_target_pairs={{0,1},{1,0},{2,3},{3,2},{4,5},{5,4},{6,7},{7,6},{8,9},{9,8},{10,11... | collective-permute-start | bytes 983048 | tf_op jit(solution)/shard_map/ppermute | solution.py:13
  16.3 19.7 %collective-permute-start = (f32[4]{0:T(128)S(1)}, f32[4]{0:T(128)S(1)}, u32[]{:S(2)}, u32[]{:S(2)}) collective-permute-start(f32[4]{0:T(128)S(1)} %select_convert_fusion.1), channel_id=1, source_target_pairs={{0,1},{1,0},{2,3},{3,2},{4,5},{5,4},{6,7},{7,6},{8,9},{9,8},{10,11... | collective-permute-start | bytes 56 | tf_op jit(solution)/shard_map/ppermute | solution.py:13
  33.9 0.9 copy-start.2
  42.5 4.6 %collective-permute-start.3 = (f32[4]{0:T(128)S(1)}, f32[4]{0:T(128)S(1)}, u32[]{:S(2)}, u32[]{:S(2)}) collective-permute-start(f32[4]{0:T(128)S(1)} %select_convert_fusion), channel_id=1, source_target_pairs={{0,2},{1,3},{2,0},{3,1},{4,6},{5,7},{6,4},{7,5},{8,10},{9,11},{10,... | collective-permute-start | bytes 56 | tf_op jit(solution)/shard_map/ppermute | solution.py:13
  58.2 71.0 %collective-permute-start.2 = (f32[4,5,4096]{2,1,0:T(8,128)}, f32[4,5,4096]{2,1,0:T(8,128)S(1)}, u32[]{:S(2)}, u32[]{:S(2)}) collective-permute-start(f32[4,5,4096]{2,1,0:T(8,128)} %broadcast_select_fusion), channel_id=1, source_target_pairs={{0,2},{1,3},{2,0},{3,1},{4,6},{5,7},{6,4},{7,5},{8,10},{9,11},{10,... | collective-permute-start | bytes 983048 | tf_op jit(solution)/shard_map/ppermute | solution.py:13
Sparse Core Ops, SparseCore 0:
  47.0 70.3 all-reduce.2
where the time goes:
time: 144 us; the launch traced here: 143 us
  waiting for transfers between devices  57.3 us (40%)
  other arithmetic  30.1 us (21%)
  local copies, waits for them, and re-layouts  20.8 us (14%)
  between operations  17.4 us (12%)
  blocking collectives  10.3 us (7%)
  starting transfers between devices  5.65 us (4%)
    unnamed x2, waiting for transfers between devices  57.2 us
    reduce_sum x1, other arithmetic, restrict(): jnp.mean(blocks, axis=(-5, -3, -1))  10.6 us
    psum x1, blocking collectives, parent_sums(): group_sums = lax.psum(level_sums, 'bal')  10.3 us
    select_n x2, other arithmetic, place_rows(): jnp.where(is_kept[:, None, None], fine_rows, jnp.where(is_hit[:, None, No...  6.28 us
    select_n x1, local copies, waits for them, and re-layouts, per_device(): fine_rows = jnp.where(is_kept[:, None, None], patches, 0.0)  6.24 us
    ppermute x4, starting transfers between devices, from_partner(): lax.ppermute(array, axis, [(i, i ^ 1 << stride) for i in range(lax.axis_s...  5.62 us
    gather x2, local copies, waits for them, and re-layouts, place_rows(): in_rows[place_index]  4.45 us
    unnamed x10, local copies, waits for them, and re-layouts  4.34 us
  transfers between devices with their start and end apart: 5, of which 2 were waited for; matrix products, arithmetic and copies ran while one was open for 28% of the time, Pallas kernels for 0%

commit v1 on v0

v1 whole, which is shorter than its diff:
```python
import functools

import jax
import jax.numpy as jnp
from jax import lax
from jax.experimental import pallas as pl
from jax.experimental.pallas import tpu as pltpu
from jax.sharding import PartitionSpec as P

EDGE = 16
SEND_MOST = 4
PAR_DEV = 2
LANES = 128
ROWS = 8
MESH = pl.DeviceIdType.MESH


def pool_matrix():
    plane, half = EDGE * EDGE, EDGE // 2
    fine = lax.broadcasted_iota(jnp.int32, (2 * plane, half * half * 2), 0)
    coarse = lax.broadcasted_iota(jnp.int32, (2 * plane, half * half * 2), 1)
    same_z = (fine // plane) == (coarse // (half * half))
    same_y = ((fine % plane) // (2 * EDGE)) == ((coarse % (half * half)) // half)
    same_x = ((fine % EDGE) // 2) == (coarse % half)
    return jnp.where(same_z & same_y & same_x, 1.0, 0.0).astype(jnp.bfloat16)


def split(x):
    high = x.astype(jnp.bfloat16)
    low = (x - high.astype(jnp.float32)).astype(jnp.bfloat16)
    return high, low


def kernel(
    group, levels, rounds,
    x_ref, ids_ref, live_ref, counts_ref, parent_ref,
    out_ref, new_ids_ref, coarse_ref,
    work, result, out_rows, in_rows, out_marks, in_marks,
    part, part_in, held, held_in, gathered,
    read_sem, write_sem, row_send, row_recv, mark_send, mark_recv,
    a_send, a_recv, b_send, b_recv, c_send, c_recv,
):
    variables, capacity, cells = x_ref.shape
    first_rows = -(-(capacity - SEND_MOST * rounds) // ROWS) * ROWS
    tiles_per = gathered.shape[1]
    bal = lax.axis_index("bal")
    level = lax.axis_index("level")

    def partner(r):
        step = 1 << r
        return bal + step * (1 - 2 * ((bal // step) % 2))

    reads = [
        pltpu.make_async_copy(
            x_ref.at[v, pl.ds(0, first_rows)], work.at[v, pl.ds(0, first_rows)], read_sem.at[v]
        )
        for v in range(variables)
    ]
    for read in reads:
        read.start()

    barrier = pltpu.get_barrier_semaphore()
    for d in range(1, group):
        pl.semaphore_signal(barrier, inc=1, device_id={"bal": lax.rem(bal + d, group)}, device_id_type=MESH)
    for d in range(1, levels):
        pl.semaphore_signal(barrier, inc=1, device_id={"level": lax.rem(level + d, levels)}, device_id_type=MESH)

    lane = lax.broadcasted_iota(jnp.int32, (ROWS, LANES), 1)
    marks = jnp.full((ROWS, LANES), -1, jnp.int32)
    parent = jnp.full((ROWS, LANES), -1, jnp.int32)
    live = live_ref[0]
    known = parent_ref.shape[0] - 1
    for s in range(capacity):
        mark = ids_ref[s]
        marks = jnp.where(lane == s, mark, marks)
        if s < first_rows:
            parent = jnp.where(lane == s, parent_ref[jnp.clip(mark, 0, known)], parent)
    parent = jnp.where(lane < live, parent, -1)

    pl.semaphore_wait(barrier, group - 1 + levels - 1)

    width = 512
    half = cells // 2
    chunks = half // width
    row = lax.broadcasted_iota(jnp.int32, (ROWS, width), 0)

    def send_rows(r, v):
        return pltpu.make_async_remote_copy(
            src_ref=out_rows.at[r, v], dst_ref=in_rows.at[r, v],
            send_sem=row_send.at[r, v], recv_sem=row_recv.at[r, v],
            device_id={"bal": partner(r)}, device_id_type=MESH,
        )

    def send_marks(r):
        return pltpu.make_async_remote_copy(
            src_ref=out_marks.at[r], dst_ref=in_marks.at[r],
            send_sem=mark_send.at[r], recv_sem=mark_recv.at[r],
            device_id={"bal": partner(r)}, device_id_type=MESH,
        )

    def post_marks(r, marks, held_count, sent):
        start = held_count - sent
        moved = pltpu.roll(marks, lax.rem(LANES - start, LANES), 1)
        out_marks[r] = jnp.where(lane < sent, moved, -1)
        send_marks(r).start()

    def take_marks(r, marks, kept):
        send_marks(r).wait_recv()
        arrived = in_marks[r]
        count = jnp.sum(jnp.where(arrived[0:1] >= 0, 1, 0))
        moved = pltpu.roll(arrived, kept, 1)
        marks = jnp.where(lane < kept, marks, jnp.where(lane < kept + count, moved, -1))
        return marks, count

    def tile_count(r):
        return -(-(capacity - SEND_MOST * (rounds - r)) // ROWS)

    def pack(r, tiles_low, tiles_high, start, stop):
        def window(tiles, shift):
            picked = tiles[0]
            for t in range(1, len(tiles)):
                slot = row + t * ROWS
                picked = jnp.where((slot >= start) & (slot < stop), tiles[t], picked)
            return pltpu.roll(picked, shift, 0)

        back = lax.rem(8 * ROWS - start, ROWS)
        low = window(tiles_low, back)
        high = window(tiles_high, lax.rem(back + SEND_MOST, ROWS))
        return jnp.where(row < SEND_MOST, low, high)

    def load(v, t, lanes):
        return work[v, pl.ds(t * ROWS, ROWS), lanes]

    def lanes_of(c):
        low = pl.multiple_of(c * width, LANES)
        high = pl.multiple_of(half + c * width, LANES)
        return pl.ds(low, width), pl.ds(high, width)

    def merge(tiles, t_count, arrived, kept, count, is_high):
        shift = lax.rem(kept + (SEND_MOST if is_high else 0), ROWS)
        moved = pltpu.roll(arrived, shift, 0)
        merged = []
        for t in range(t_count):
            slot = row + t * ROWS
            fresh = jnp.where((slot >= kept) & (slot < kept + count), moved, 0.0)
            merged.append(jnp.where(slot < kept, tiles[t], fresh) if t < len(tiles) else fresh)
        return merged

    sent = counts_ref[0, 0]
    post_marks(0, marks, live, sent)
    for v in range(variables):
        reads[v].wait()

        def body(c, carry, v=v):
            low, high = lanes_of(c)
            count = tile_count(0)
            out_rows[0, v, :, low] = pack(
                0, [load(v, t, low) for t in range(count)],
                [load(v, t, high) for t in range(count)], live - sent, live,
            )
            return carry

        lax.fori_loop(0, chunks, body, 0)
        send_rows(0, v).start()

    pool = pool_matrix()
    parents = levels * PAR_DEV
    one_row = lax.broadcasted_iota(jnp.int32, (parents, first_rows), 0)
    one_hot = jnp.where(one_row == parent[0:1, :first_rows], 1.0, 0.0).astype(jnp.bfloat16)
    both_hot = jnp.concatenate([one_hot, one_hot], axis=1)
    plane = EDGE * EDGE
    quarters = cells // (4 * plane)
    slot_of = lax.broadcasted_iota(jnp.int32, (first_rows, plane), 0)
    for v in range(variables):
        rows = []
        for q in range(quarters):
            sums = []
            for k in (2 * q, 2 * q + 1):
                a = work[v, 0:first_rows, 2 * k * plane:(2 * k + 1) * plane]
                b = work[v, 0:first_rows, (2 * k + 1) * plane:(2 * k + 2) * plane]
                sums.append(jnp.where(slot_of < live, a + b, 0.0))
            rows.extend(split(jnp.concatenate(sums, axis=1)))
        pooled = jnp.dot(jnp.concatenate(rows, axis=0), pool, preferred_element_type=jnp.float32)
        for q in range(quarters):
            base = 2 * q * first_rows
            mean = 0.125 * (pooled[base:base + first_rows] + pooled[base + first_rows:base + 2 * first_rows])
            total = jnp.dot(
                both_hot, jnp.concatenate(split(mean), axis=0), preferred_element_type=jnp.float32
            )
            k = v * quarters + q
            for m in range(levels):
                part[k // tiles_per, m, k % tiles_per] = total[PAR_DEV * m:PAR_DEV * (m + 1)]
    for k in range(variables * quarters, group * tiles_per):
        part[k // tiles_per, :, k % tiles_per] = jnp.zeros((levels, PAR_DEV, LANES), jnp.float32)

    def send_a(d):
        to = lax.rem(bal + d, group)
        return pltpu.make_async_remote_copy(
            src_ref=part.at[to], dst_ref=part_in.at[d - 1],
            send_sem=a_send.at[d - 1], recv_sem=a_recv.at[d - 1],
            device_id={"bal": to}, device_id_type=MESH,
        )

    def send_b(d):
        to = lax.rem(level + d, levels)
        return pltpu.make_async_remote_copy(
            src_ref=held.at[to], dst_ref=held_in.at[d - 1],
            send_sem=b_send.at[d - 1], recv_sem=b_recv.at[d - 1],
            device_id={"level": to}, device_id_type=MESH,
        )

    def send_c(d):
        to = lax.rem(bal + d, group)
        return pltpu.make_async_remote_copy(
            src_ref=gathered.at[bal], dst_ref=gathered.at[bal],
            send_sem=c_send.at[d - 1], recv_sem=c_recv.at[d - 1],
            device_id={"bal": to}, device_id_type=MESH,
        )

    for d in range(1, group):
        send_a(d).start()

    held_count = live
    for r in range(1, rounds):
        kept = held_count - sent
        marks, count = take_marks(r - 1, marks, kept)
        held_count = kept + count
        sent = counts_ref[r, 0]
        post_marks(r, marks, held_count, sent)
        for v in range(variables):
            send_rows(r - 1, v).wait_recv()

            def body(c, carry, v=v, r=r, kept=kept, count=count, held_count=held_count, sent=sent):
                lanes = lanes_of(c)
                arrived = in_rows[r - 1, v, :, lanes[0]]
                merged = []
                for i in range(2):
                    tiles = [load(v, t, lanes[i]) for t in range(tile_count(r - 1))]
                    merged.append(merge(tiles, tile_count(r), arrived, kept, count, i == 1))
                    for t in range(tile_count(r)):
                        work[v, pl.ds(t * ROWS, ROWS), lanes[i]] = merged[i][t]
                out_rows[r, v, :, lanes[0]] = pack(
                    r, merged[0], merged[1], held_count - sent, held_count
                )
                return carry

            lax.fori_loop(0, chunks, body, 0)
            send_rows(r, v).start()

    for d in range(1, group):
        send_a(d).wait_recv()

    def add_a(m, carry):
        total = part[bal, m]
        for d in range(1, group):
            total = total + part_in[d - 1, m]
        held[m] = total
        return carry

    lax.fori_loop(0, levels, add_a, 0)
    for d in range(1, levels):
        send_b(d).start()
    for d in range(1, levels):
        send_b(d).wait_recv()
    total = held[level]
    for d in range(1, levels):
        total = total + held_in[d - 1]
    gathered[bal] = total
    for d in range(1, group):
        send_c(d).start()

    kept = held_count - sent
    marks, count = take_marks(rounds - 1, marks, kept)
    new_ids_ref[...] = marks[0:1]
    writes = []
    for v in range(variables):
        send_rows(rounds - 1, v).wait_recv()

        def body(c, carry, v=v):
            lanes = lanes_of(c)
            arrived = in_rows[rounds - 1, v, :, lanes[0]]
            for i in range(2):
                tiles = [load(v, t, lanes[i]) for t in range(tile_count(rounds - 1))]
                merged = merge(tiles, tile_count(rounds), arrived, kept, count, i == 1)
                for t in range(tile_count(rounds)):
                    size = min(ROWS, capacity - t * ROWS)
                    result[v, pl.ds(t * ROWS, size), lanes[i]] = merged[t][0:size]
            return carry

        lax.fori_loop(0, chunks, body, 0)
        writes.append(pltpu.make_async_copy(result.at[v], out_ref.at[v], write_sem.at[v]))
        writes[-1].start()

    for d in range(1, group):
        send_c(d).wait_recv()
    for k in range(variables * quarters):
        v, q = k // quarters, k % quarters
        coarse_ref[v, :, q * LANES:(q + 1) * LANES] = gathered[k // tiles_per, k % tiles_per]

    for r in range(rounds):
        send_marks(r).wait_send()
        for v in range(variables):
            send_rows(r, v).wait_send()
    for d in range(1, group):
        send_a(d).wait_send()
        send_c(d).wait_send()
    for d in range(1, levels):
        send_b(d).wait_send()
    for write in writes:
        write.wait()


def per_device(patches, patch_ids, live, counts, parent_of):
    capacity, variables, cells = patches.shape
    group = lax.axis_size("bal")
    levels = lax.axis_size("level")
    rounds = counts.shape[0]
    coarse_cells = cells // 8
    tiles_per = -(-(variables * coarse_cells // LANES) // group)
    padded = -(-capacity // ROWS) * ROWS
    f32 = jnp.float32
    dma = pltpu.SemaphoreType.DMA
    fine, ids, coarse = pl.pallas_call(
        functools.partial(kernel, group, levels, rounds),
        out_shape=(
            jax.ShapeDtypeStruct((variables, capacity, cells), f32),
            jax.ShapeDtypeStruct((1, LANES), jnp.int32),
            jax.ShapeDtypeStruct((variables, PAR_DEV, coarse_cells), f32),
        ),
        in_specs=[
            pl.BlockSpec(memory_space=pl.ANY),
            pl.BlockSpec(memory_space=pltpu.SMEM),
            pl.BlockSpec(memory_space=pltpu.SMEM),
            pl.BlockSpec(memory_space=pltpu.SMEM),
            pl.BlockSpec(memory_space=pltpu.SMEM),
        ],
        out_specs=(
            pl.BlockSpec(memory_space=pl.ANY),
            pl.BlockSpec(memory_space=pltpu.VMEM),
            pl.BlockSpec(memory_space=pltpu.VMEM),
        ),
        scratch_shapes=[
            pltpu.VMEM((variables, padded, cells), f32),
            pltpu.VMEM((variables, capacity, cells), f32),
            pltpu.VMEM((rounds, variables, ROWS, cells // 2), f32),
            pltpu.VMEM((rounds, variables, ROWS, cells // 2), f32),
            pltpu.VMEM((rounds, ROWS, LANES), jnp.int32),
            pltpu.VMEM((rounds, ROWS, LANES), jnp.int32),
            pltpu.VMEM((group, levels, tiles_per, PAR_DEV, LANES), f32),
            pltpu.VMEM((group - 1, levels, tiles_per, PAR_DEV, LANES), f32),
            pltpu.VMEM((levels, tiles_per, PAR_DEV, LANES), f32),
            pltpu.VMEM((levels - 1, tiles_per, PAR_DEV, LANES), f32),
            pltpu.VMEM((group, tiles_per, PAR_DEV, LANES), f32),
            dma((variables,)),
            dma((variables,)),
            dma((rounds, variables)),
            dma((rounds, variables)),
            dma((rounds,)),
            dma((rounds,)),
            dma((group - 1,)),
            dma((group - 1,)),
            dma((levels - 1,)),
            dma((levels - 1,)),
            dma((group - 1,)),
            dma((group - 1,)),
        ],
        compiler_params=pltpu.CompilerParams(collective_id=0, has_side_effects=True),
    )(patches.transpose(1, 0, 2), patch_ids, live, counts, parent_of)
    return (fine.transpose(1, 0, 2), ids[0, :capacity], coarse.transpose(1, 0, 2))


def solution(mesh):
    return jax.shard_map(
        per_device,
        mesh=mesh,
        in_specs=(
            P(("level", "bal"), None, None),
            P(("level", "bal")),
            P(("level", "bal")),
            P(None, ("level", "bal")),
            P(),
        ),
        out_specs=(P(("level", "bal"), None, None), P(("level", "bal")), P("level", None, None)),
        check_vma=False,
    )
```

time: 144 us -> 28.6 us (0.20)
  waiting for transfers between devices: 57.3 us -> 0 us
  other arithmetic: 30.1 us -> 0 us
  Pallas kernels: 0 us -> 21 us
  between operations: 17.4 us -> 1.29 us
  local copies, waits for them, and re-layouts: 20.8 us -> 6.08 us
  blocking collectives: 10.3 us -> 0 us
  starting transfers between devices: 5.65 us -> 0 us
    unnamed x2 -> x0, waiting for transfers between devices: 57.2 us -> none
    pallas_call x0 -> x1, Pallas kernels: none -> 21 us  [per_device(): pl.pallas_call(functools.partial(kernel, group, levels, rounds), out_shap...]
    select_n x12 -> x0, other arithmetic: 16.3 us -> none  [the longest x2 6.28 us: place_rows(): jnp.where(is_kept[:, None, None], fine_rows, jnp.where(is_hit[:, None, No...]
    reduce_sum x2 -> x0, other arithmetic: 11.2 us -> none  [the longest x1 10.6 us: restrict(): jnp.mean(blocks, axis=(-5, -3, -1))]
    psum x1 -> x0, blocking collectives: 10.3 us -> none  [parent_sums(): group_sums = lax.psum(level_sums, 'bal')]
    gather x9 -> x0, local copies, waits for them, and re-layouts: 8.91 us -> none  [the longest x2 4.45 us: place_rows(): in_rows[place_index]]
    select_n x1 -> x0, local copies, waits for them, and re-layouts: 6.24 us -> none  [per_device(): fine_rows = jnp.where(is_kept[:, None, None], patches, 0.0)]
    ppermute x4 -> x0, starting transfers between devices: 5.62 us -> none  [from_partner(): lax.ppermute(array, axis, [(i, i ^ 1 << stride) for i in range(lax.axis_s...]
  transfers between devices with their start and end apart: 5 -> 0, of which waited for: 2 -> 0; matrix products, arithmetic and copies ran while one was open for 28% -> 0% of each run, Pallas kernels for 0% -> 0%
where the time goes in v1:
time: 28.6 us; the launch traced here: 28.4 us
  Pallas kernels  21 us (73%)
  local copies, waits for them, and re-layouts  6.08 us (21%)
  between operations  1.29 us (5%)
    pallas_call x1, Pallas kernels, per_device(): pl.pallas_call(functools.partial(kernel, group, levels, rounds), out_shap...  21 us
    unnamed x5, local copies, waits for them, and re-layouts  4.91 us
    squeeze x1, local copies, waits for them, and re-layouts, per_device(): ids[0, :capacity]  1.17 us

profile of v1, /device:TPU:0, one launch (start us, length us, event | category | flops | bytes accessed | tf_op | source)
XLA Modules:
  0.0 28.4 jit_solution(5994183064045531275)
XLA Ops:
  1.3 1.3 %copy.8.counts_ref = s32[2,1]{1,0:T(2,128)} copy(s32[2,1]{0,1:T(1,128)} %param.8) | data formatting | bytes 16 | tf_op args[3]
  2.6 21.0 %shard_map.76 = (f32[5,20,4096]{2,1,0:T(8,128)}, s32[1,128]{1,0:T(1,128)}, f32[5,2,512]{2,1,0:T(2,128)}) custom-call(f32[5,20,4096]{2,1,0:T(8,128)} %bitcast.5, s32[20]{0:T(128)} %ids_ref.1, s32[1]{0:T(128)S(6)} %copy.11.live_ref, s32[2,1]{1,0:T(2,128)} %copy.8.counts_ref, s32[640]{0:T(1024)} %parent_ref.1), custom_call_target="tpu_custom_call" | custom-call | tf_op jit(solution)/shard_map/pallas_call | solution.py:323
  23.6 1.2 %slice_bitcast_fusion = s32[20]{0:T(128)} fusion(s32[1,128]{1,0:T(1,128)} %get-tuple-element.7), kind=kLoop, calls=%fused_computation | loop fusion | bytes 160 | tf_op jit(solution)/shard_map/squeeze | solution.py:369
  24.7 0.0 copy-start
  24.7 3.0 %copy.12 = f32[20,5,4096]{2,0,1:T(8,128)} copy(f32[20,5,4096]{2,0,1:T(8,128)} %bitcast.6) | data formatting | bytes 3276800
  27.8 0.0 copy-done
  27.8 0.6 %copy.13 = f32[2,5,512]{2,0,1:T(2,128)} copy(f32[2,5,512]{2,0,1:T(2,128)S(1)} %bitcast.7) | data formatting | bytes 40960
Async XLA Ops:
  24.7 3.0 %copy-start = (f32[5,2,512]{2,1,0:T(2,128)S(1)}, f32[5,2,512]{2,1,0:T(2,128)}, u32[]{:S(2)}) copy-start(f32[5,2,512]{2,1,0:T(2,128)} %get-tuple-element.8) | copy-start | bytes 61444

commit v2 on v1

--- a/solution.py
+++ b/solution.py
@@ -11,6 +11,7 @@
 SEND_MOST = 4
 PAR_DEV = 2
 LANES = 128
+AHEAD = 2
 ROWS = 8
 MESH = pl.DeviceIdType.MESH
 
@@ -33,16 +34,15 @@
 
 def kernel(
     group, levels, rounds,
-    x_ref, ids_ref, live_ref, counts_ref, parent_ref,
+    x_ref, ids_ref, live_ref, counts_in, parent_ref,
     out_ref, new_ids_ref, coarse_ref,
     work, result, out_rows, in_rows, out_marks, in_marks,
-    part, part_in, held, held_in, gathered,
-    read_sem, write_sem, row_send, row_recv, mark_send, mark_recv,
-    a_send, a_recv, b_send, b_recv, c_send, c_recv,
+    part, part_in, gathered, counts_ref, ids, parents_of,
+    read_sem, small_sem, write_sem, row_send, row_recv, mark_send, mark_recv,
+    a_send, a_recv, b_send, b_recv,
 ):
     variables, capacity, cells = x_ref.shape
     first_rows = -(-(capacity - SEND_MOST * rounds) // ROWS) * ROWS
-    tiles_per = gathered.shape[1]
     bal = lax.axis_index("bal")
     level = lax.axis_index("level")
 
@@ -52,12 +52,17 @@
 
     reads = [
         pltpu.make_async_copy(
-            x_ref.at[v, pl.ds(0, first_rows)], work.at[v, pl.ds(0, first_rows)], read_sem.at[v]
+            x_ref.at[v, pl.ds(0, first_rows)], work.at[0, v, pl.ds(0, first_rows)], read_sem.at[v]
         )
         for v in range(variables)
     ]
-    for read in reads:
-        read.start()
+    small = [
+        pltpu.make_async_copy(counts_in, counts_ref, small_sem.at[0]),
+        pltpu.make_async_copy(ids_ref, ids, small_sem.at[1]),
+        pltpu.make_async_copy(parent_ref, parents_of, small_sem.at[2]),
+    ]
+    for copy in small[:1] + reads[:1] + small[1:] + reads[1:]:
+        copy.start()
 
     barrier = pltpu.get_barrier_semaphore()
     for d in range(1, group):
@@ -66,19 +71,8 @@
         pl.semaphore_signal(barrier, inc=1, device_id={"level": lax.rem(level + d, levels)}, device_id_type=MESH)
 
     lane = lax.broadcasted_iota(jnp.int32, (ROWS, LANES), 1)
-    marks = jnp.full((ROWS, LANES), -1, jnp.int32)
-    parent = jnp.full((ROWS, LANES), -1, jnp.int32)
+    small[0].wait()
     live = live_ref[0]
-    known = parent_ref.shape[0] - 1
-    for s in range(capacity):
-        mark = ids_ref[s]
-        marks = jnp.where(lane == s, mark, marks)
-        if s < first_rows:
-            parent = jnp.where(lane == s, parent_ref[jnp.clip(mark, 0, known)], parent)
-    parent = jnp.where(lane < live, parent, -1)
-
-    pl.semaphore_wait(barrier, group - 1 + levels - 1)
-
     width = 512
     half = cells // 2
     chunks = half // width
@@ -128,8 +122,8 @@
         high = window(tiles_high, lax.rem(back + SEND_MOST, ROWS))
         return jnp.where(row < SEND_MOST, low, high)
 
-    def load(v, t, lanes):
-        return work[v, pl.ds(t * ROWS, ROWS), lanes]
+    def load(r, v, t, lanes):
+        return work[r, v, pl.ds(t * ROWS, ROWS), lanes]
 
     def lanes_of(c):
         low = pl.multiple_of(c * width, LANES)
@@ -146,8 +140,7 @@
             merged.append(jnp.where(slot < kept, tiles[t], fresh) if t < len(tiles) else fresh)
         return merged
 
-    sent = counts_ref[0, 0]
-    post_marks(0, marks, live, sent)
+    sent = counts_ref[0]
     for v in range(variables):
         reads[v].wait()
 
@@ -155,13 +148,28 @@
             low, high = lanes_of(c)
             count = tile_count(0)
             out_rows[0, v, :, low] = pack(
-                0, [load(v, t, low) for t in range(count)],
-                [load(v, t, high) for t in range(count)], live - sent, live,
+                0, [load(0, v, t, low) for t in range(count)],
+                [load(0, v, t, high) for t in range(count)], live - sent, live,
             )
             return carry
 
         lax.fori_loop(0, chunks, body, 0)
+        if v == 0:
+            pl.semaphore_wait(barrier, group - 1 + levels - 1)
         send_rows(0, v).start()
+        if v == 0:
+            for copy in small[1:]:
+                copy.wait()
+            marks = jnp.full((ROWS, LANES), -1, jnp.int32)
+            for s in range(capacity):
+                marks = jnp.where(lane == s, ids[s], marks)
+            post_marks(0, marks, live, sent)
+
+    parent = jnp.full((ROWS, LANES), -1, jnp.int32)
+    for s in range(first_rows):
+        mine = parents_of[jnp.clip(ids[s], 0, parents_of.shape[0] - 1)]
+        parent = jnp.where(lane == s, mine, parent)
+    parent = jnp.where(lane < live, parent, -1)
 
     pool = pool_matrix()
     parents = levels * PAR_DEV
@@ -171,13 +179,13 @@
     plane = EDGE * EDGE
     quarters = cells // (4 * plane)
     slot_of = lax.broadcasted_iota(jnp.int32, (first_rows, plane), 0)
-    for v in range(variables):
+    def restrict_rows(v):
         rows = []
         for q in range(quarters):
             sums = []
             for k in (2 * q, 2 * q + 1):
-                a = work[v, 0:first_rows, 2 * k * plane:(2 * k + 1) * plane]
-                b = work[v, 0:first_rows, (2 * k + 1) * plane:(2 * k + 2) * plane]
+                a = work[0, v, 0:first_rows, 2 * k * plane:(2 * k + 1) * plane]
+                b = work[0, v, 0:first_rows, (2 * k + 1) * plane:(2 * k + 2) * plane]
                 sums.append(jnp.where(slot_of < live, a + b, 0.0))
             rows.extend(split(jnp.concatenate(sums, axis=1)))
         pooled = jnp.dot(jnp.concatenate(rows, axis=0), pool, preferred_element_type=jnp.float32)
@@ -187,47 +195,42 @@
             total = jnp.dot(
                 both_hot, jnp.concatenate(split(mean), axis=0), preferred_element_type=jnp.float32
             )
-            k = v * quarters + q
             for m in range(levels):
-                part[k // tiles_per, m, k % tiles_per] = total[PAR_DEV * m:PAR_DEV * (m + 1)]
-    for k in range(variables * quarters, group * tiles_per):
-        part[k // tiles_per, :, k % tiles_per] = jnp.zeros((levels, PAR_DEV, LANES), jnp.float32)
+                part[m, v, :, q * LANES:(q + 1) * LANES] = total[PAR_DEV * m:PAR_DEV * (m + 1)]
+
 
     def send_a(d):
-        to = lax.rem(bal + d, group)
+        to = lax.rem(level + d, levels)
         return pltpu.make_async_remote_copy(
             src_ref=part.at[to], dst_ref=part_in.at[d - 1],
             send_sem=a_send.at[d - 1], recv_sem=a_recv.at[d - 1],
-            device_id={"bal": to}, device_id_type=MESH,
+            device_id={"level": to}, device_id_type=MESH,
         )
 
     def send_b(d):
-        to = lax.rem(level + d, levels)
-        return pltpu.make_async_remote_copy(
-            src_ref=held.at[to], dst_ref=held_in.at[d - 1],
-            send_sem=b_send.at[d - 1], recv_sem=b_recv.at[d - 1],
-            device_id={"level": to}, device_id_type=MESH,
-        )
-
-    def send_c(d):
         to = lax.rem(bal + d, group)
         return pltpu.make_async_remote_copy(
             src_ref=gathered.at[bal], dst_ref=gathered.at[bal],
-            send_sem=c_send.at[d - 1], recv_sem=c_recv.at[d - 1],
+            send_sem=b_send.at[d - 1], recv_sem=b_recv.at[d - 1],
             device_id={"bal": to}, device_id_type=MESH,
         )
 
-    for d in range(1, group):
-        send_a(d).start()
+    def parent_sums():
+        for v in range(variables):
+            restrict_rows(v)
+        for d in range(1, levels):
+            send_a(d).start()
 
     held_count = live
     for r in range(1, rounds):
         kept = held_count - sent
         marks, count = take_marks(r - 1, marks, kept)
         held_count = kept + count
-        sent = counts_ref[r, 0]
+        sent = counts_ref[r]
         post_marks(r, marks, held_count, sent)
         for v in range(variables):
+            if r == 1 and v == AHEAD:
+                parent_sums()
             send_rows(r - 1, v).wait_recv()
 
             def body(c, carry, v=v, r=r, kept=kept, count=count, held_count=held_count, sent=sent):
@@ -235,10 +238,10 @@
                 arrived = in_rows[r - 1, v, :, lanes[0]]
                 merged = []
                 for i in range(2):
-                    tiles = [load(v, t, lanes[i]) for t in range(tile_count(r - 1))]
+                    tiles = [load(r - 1, v, t, lanes[i]) for t in range(tile_count(r - 1))]
                     merged.append(merge(tiles, tile_count(r), arrived, kept, count, i == 1))
                     for t in range(tile_count(r)):
-                        work[v, pl.ds(t * ROWS, ROWS), lanes[i]] = merged[i][t]
+                        work[r, v, pl.ds(t * ROWS, ROWS), lanes[i]] = merged[i][t]
                 out_rows[r, v, :, lanes[0]] = pack(
                     r, merged[0], merged[1], held_count - sent, held_count
                 )
@@ -247,27 +250,14 @@
             lax.fori_loop(0, chunks, body, 0)
             send_rows(r, v).start()
 
-    for d in range(1, group):
+    for d in range(1, levels):
         send_a(d).wait_recv()
-
-    def add_a(m, carry):
-        total = part[bal, m]
-        for d in range(1, group):
-            total = total + part_in[d - 1, m]
-        held[m] = total
-        return carry
-
-    lax.fori_loop(0, levels, add_a, 0)
+    total = part[level]
     for d in range(1, levels):
-        send_b(d).start()
-    for d in range(1, levels):
-        send_b(d).wait_recv()
-    total = held[level]
-    for d in range(1, levels):
-        total = total + held_in[d - 1]
+        total = total + part_in[d - 1]
     gathered[bal] = total
     for d in range(1, group):
-        send_c(d).start()
+        send_b(d).start()
 
     kept = held_count - sent
     marks, count = take_marks(rounds - 1, marks, kept)
@@ -280,7 +270,7 @@
             lanes = lanes_of(c)
             arrived = in_rows[rounds - 1, v, :, lanes[0]]
             for i in range(2):
-                tiles = [load(v, t, lanes[i]) for t in range(tile_count(rounds - 1))]
+                tiles = [load(rounds - 1, v, t, lanes[i]) for t in range(tile_count(rounds - 1))]
                 merged = merge(tiles, tile_count(rounds), arrived, kept, count, i == 1)
                 for t in range(tile_count(rounds)):
                     size = min(ROWS, capacity - t * ROWS)
@@ -292,22 +282,26 @@
         writes[-1].start()
 
     for d in range(1, group):
-        send_c(d).wait_recv()
-    for k in range(variables * quarters):
-        v, q = k // quarters, k % quarters
-        coarse_ref[v, :, q * LANES:(q + 1) * LANES] = gathered[k // tiles_per, k % tiles_per]
+        send_b(d).wait_recv()
+    total = gathered[0]
+    for b in range(1, group):
+        total = total + gathered[b]
+    coarse_ref[...] = total
 
     for r in range(rounds):
         send_marks(r).wait_send()
         for v in range(variables):
             send_rows(r, v).wait_send()
     for d in range(1, group):
+        send_b(d).wait_send()
+    for d in range(1, levels):
         send_a(d).wait_send()
-        send_c(d).wait_send()
-    for d in range(1, levels):
-        send_b(d).wait_send()
     for write in writes:
         write.wait()
+
+
+def hbm(x):
+    return pltpu.with_memory_space_constraint(x, pltpu.HBM)
 
 
 def per_device(patches, patch_ids, live, counts, parent_of):
@@ -316,7 +310,6 @@
     levels = lax.axis_size("level")
     rounds = counts.shape[0]
     coarse_cells = cells // 8
-    tiles_per = -(-(variables * coarse_cells // LANES) // group)
     padded = -(-capacity // ROWS) * ROWS
     f32 = jnp.float32
     dma = pltpu.SemaphoreType.DMA
@@ -328,11 +321,11 @@
             jax.ShapeDtypeStruct((variables, PAR_DEV, coarse_cells), f32),
         ),
         in_specs=[
-            pl.BlockSpec(memory_space=pl.ANY),
+            pl.BlockSpec(memory_space=pltpu.HBM),
+            pl.BlockSpec(memory_space=pltpu.HBM),
             pl.BlockSpec(memory_space=pltpu.SMEM),
-            pl.BlockSpec(memory_space=pltpu.SMEM),
-            pl.BlockSpec(memory_space=pltpu.SMEM),
-            pl.BlockSpec(memory_space=pltpu.SMEM),
+            pl.BlockSpec(memory_space=pltpu.HBM),
+            pl.BlockSpec(memory_space=pltpu.HBM),
         ],
         out_specs=(
             pl.BlockSpec(memory_space=pl.ANY),
@@ -340,32 +333,32 @@
             pl.BlockSpec(memory_space=pltpu.VMEM),
         ),
         scratch_shapes=[
-            pltpu.VMEM((variables, padded, cells), f32),
+            pltpu.VMEM((rounds, variables, padded, cells), f32),
             pltpu.VMEM((variables, capacity, cells), f32),
             pltpu.VMEM((rounds, variables, ROWS, cells // 2), f32),
             pltpu.VMEM((rounds, variables, ROWS, cells // 2), f32),
             pltpu.VMEM((rounds, ROWS, LANES), jnp.int32),
             pltpu.VMEM((rounds, ROWS, LANES), jnp.int32),
-            pltpu.VMEM((group, levels, tiles_per, PAR_DEV, LANES), f32),
-            pltpu.VMEM((group - 1, levels, tiles_per, PAR_DEV, LANES), f32),
-            pltpu.VMEM((levels, tiles_per, PAR_DEV, LANES), f32),
-            pltpu.VMEM((levels - 1, tiles_per, PAR_DEV, LANES), f32),
-            pltpu.VMEM((group, tiles_per, PAR_DEV, LANES), f32),
+            pltpu.VMEM((levels, variables, PAR_DEV, coarse_cells), f32),
+            pltpu.VMEM((levels - 1, variables, PAR_DEV, coarse_cells), f32),
+            pltpu.VMEM((group, variables, PAR_DEV, coarse_cells), f32),
+            pltpu.SMEM((rounds,), jnp.int32),
+            pltpu.SMEM(patch_ids.shape, jnp.int32),
+            pltpu.SMEM(parent_of.shape, jnp.int32),
             dma((variables,)),
+            dma((3,)),
             dma((variables,)),
             dma((rounds, variables)),
             dma((rounds, variables)),
             dma((rounds,)),
             dma((rounds,)),
-            dma((group - 1,)),
-            dma((group - 1,)),
             dma((levels - 1,)),
             dma((levels - 1,)),
             dma((group - 1,)),
             dma((group - 1,)),
         ],
-        compiler_params=pltpu.CompilerParams(collective_id=0, has_side_effects=True),
-    )(patches.transpose(1, 0, 2), patch_ids, live, counts, parent_of)
+        compiler_params=pltpu.CompilerParams(collective_id=0, has_side_effects=True, vmem_limit_bytes=24 << 20),
+    )(hbm(patches.transpose(1, 0, 2)), hbm(patch_ids), live, hbm(counts.reshape(rounds)), hbm(parent_of))
     return (fine.transpose(1, 0, 2), ids[0, :capacity], coarse.transpose(1, 0, 2))
 
 

time: 28.6 us -> 21.8 us (0.76)
  local copies, waits for them, and re-layouts: 6.08 us -> 2.39 us
  Pallas kernels: 21 us -> 18 us
    unnamed x5 -> x2, local copies, waits for them, and re-layouts: 4.91 us -> 1.88 us
    pallas_call x1, Pallas kernels: 21 us -> 18 us  [per_device(): pl.pallas_call(functools.partial(kernel, group, levels, rounds), out_shap...]
    squeeze x1, local copies, waits for them, and re-layouts: 1.17 us -> 0.51 us  [per_device(): ids[0, :capacity]]
where the time goes in v2:
time: 21.8 us; the launch traced here: 21.7 us
  Pallas kernels  18 us (83%)
  local copies, waits for them, and re-layouts  2.39 us (11%)
  between operations  1.29 us (6%)
    pallas_call x1, Pallas kernels, per_device(): pl.pallas_call(functools.partial(kernel, group, levels, rounds), out_shap...  18 us
    unnamed x2, local copies, waits for them, and re-layouts  1.88 us
    squeeze x1, local copies, waits for them, and re-layouts, per_device(): ids[0, :capacity]  0.51 us

profile of v2, /device:TPU:0, one launch (start us, length us, event | category | flops | bytes accessed | tf_op | source)
XLA Modules:
  0.0 21.7 jit_solution(16732164011656950855)
XLA Ops:
  1.3 18.0 %shard_map.76 = (f32[5,20,4096]{2,1,0:T(8,128)S(1)}, s32[1,128]{1,0:T(1,128)S(1)}, f32[5,2,512]{2,1,0:T(2,128)S(1)}) custom-call(f32[5,20,4096]{2,1,0:T(8,128)} %bitcast.8, s32[20]{0:T(128)} %ids_ref.1, s32[1]{0:T(128)S(6)} %copy.10.live_ref, s32[2]{0:T(128)} %bitcast.9, s32[640]{0:T(1024)} %parent_ref.1), custom_call_target="tpu_custom_call" | custom-call | tf_op jit(solution)/shard_map/pallas_call | solution.py:316
  19.3 0.5 %slice_bitcast_fusion = s32[20]{0:T(128)} fusion(s32[1,128]{1,0:T(1,128)S(1)} %get-tuple-element.7), kind=kLoop, calls=%fused_computation | loop fusion | bytes 160 | tf_op jit(solution)/shard_map/squeeze | solution.py:362
  19.8 1.3 %copy.11 = f32[20,5,4096]{2,0,1:T(8,128)} copy(f32[20,5,4096]{2,0,1:T(8,128)S(1)} %bitcast.6) | data formatting | bytes 3276800
  21.1 0.6 %copy.12 = f32[2,5,512]{2,0,1:T(2,128)} copy(f32[2,5,512]{2,0,1:T(2,128)S(1)} %bitcast.7) | data formatting | bytes 40960

commit v3 on v2

--- a/solution.py
+++ b/solution.py
@@ -36,9 +36,9 @@
     group, levels, rounds,
     x_ref, ids_ref, live_ref, counts_in, parent_ref,
     out_ref, new_ids_ref, coarse_ref,
-    work, result, out_rows, in_rows, out_marks, in_marks,
+    work, out_rows, in_rows, out_marks, in_marks,
     part, part_in, gathered, counts_ref, ids, parents_of,
-    read_sem, small_sem, write_sem, row_send, row_recv, mark_send, mark_recv,
+    read_sem, small_sem, row_send, row_recv, mark_send, mark_recv,
     a_send, a_recv, b_send, b_recv,
 ):
     variables, capacity, cells = x_ref.shape
@@ -262,7 +262,6 @@
     kept = held_count - sent
     marks, count = take_marks(rounds - 1, marks, kept)
     new_ids_ref[...] = marks[0:1]
-    writes = []
     for v in range(variables):
         send_rows(rounds - 1, v).wait_recv()
 
@@ -274,12 +273,10 @@
                 merged = merge(tiles, tile_count(rounds), arrived, kept, count, i == 1)
                 for t in range(tile_count(rounds)):
                     size = min(ROWS, capacity - t * ROWS)
-                    result[v, pl.ds(t * ROWS, size), lanes[i]] = merged[t][0:size]
+                    out_ref[v, pl.ds(t * ROWS, size), lanes[i]] = merged[t][0:size]
             return carry
 
         lax.fori_loop(0, chunks, body, 0)
-        writes.append(pltpu.make_async_copy(result.at[v], out_ref.at[v], write_sem.at[v]))
-        writes[-1].start()
 
     for d in range(1, group):
         send_b(d).wait_recv()
@@ -296,8 +293,19 @@
         send_b(d).wait_send()
     for d in range(1, levels):
         send_a(d).wait_send()
-    for write in writes:
-        write.wait()
+
+
+def finish(fine_ref, marks_ref, sums_ref, out_ref, ids_ref, coarse_ref, sem):
+    variables = fine_ref.shape[0]
+    copies = [
+        pltpu.make_async_copy(fine_ref.at[v], out_ref.at[v], sem.at[v]) for v in range(variables)
+    ]
+    copies.append(pltpu.make_async_copy(sums_ref, coarse_ref, sem.at[variables]))
+    for copy in copies:
+        copy.start()
+    ids_ref[...] = marks_ref[0, :ids_ref.shape[0]]
+    for copy in copies:
+        copy.wait()
 
 
 def hbm(x):
@@ -328,13 +336,12 @@
             pl.BlockSpec(memory_space=pltpu.HBM),
         ],
         out_specs=(
-            pl.BlockSpec(memory_space=pl.ANY),
+            pl.BlockSpec(memory_space=pltpu.VMEM),
             pl.BlockSpec(memory_space=pltpu.VMEM),
             pl.BlockSpec(memory_space=pltpu.VMEM),
         ),
         scratch_shapes=[
             pltpu.VMEM((rounds, variables, padded, cells), f32),
-            pltpu.VMEM((variables, capacity, cells), f32),
             pltpu.VMEM((rounds, variables, ROWS, cells // 2), f32),
             pltpu.VMEM((rounds, variables, ROWS, cells // 2), f32),
             pltpu.VMEM((rounds, ROWS, LANES), jnp.int32),
@@ -347,7 +354,6 @@
             pltpu.SMEM(parent_of.shape, jnp.int32),
             dma((variables,)),
             dma((3,)),
-            dma((variables,)),
             dma((rounds, variables)),
             dma((rounds, variables)),
             dma((rounds,)),
@@ -359,7 +365,27 @@
         ],
         compiler_params=pltpu.CompilerParams(collective_id=0, has_side_effects=True, vmem_limit_bytes=24 << 20),
     )(hbm(patches.transpose(1, 0, 2)), hbm(patch_ids), live, hbm(counts.reshape(rounds)), hbm(parent_of))
-    return (fine.transpose(1, 0, 2), ids[0, :capacity], coarse.transpose(1, 0, 2))
+    fine, ids, coarse = pl.pallas_call(
+        finish,
+        out_shape=(
+            jax.ShapeDtypeStruct(fine.shape, f32),
+            jax.ShapeDtypeStruct((capacity,), jnp.int32),
+            jax.ShapeDtypeStruct(coarse.shape, f32),
+        ),
+        in_specs=[
+            pl.BlockSpec(memory_space=pl.ANY),
+            pl.BlockSpec(memory_space=pltpu.VMEM),
+            pl.BlockSpec(memory_space=pl.ANY),
+        ],
+        out_specs=(
+            pl.BlockSpec(memory_space=pl.ANY),
+            pl.BlockSpec(memory_space=pltpu.VMEM),
+            pl.BlockSpec(memory_space=pl.ANY),
+        ),
+        scratch_shapes=[dma((variables + 1,))],
+        compiler_params=pltpu.CompilerParams(vmem_limit_bytes=24 << 20),
+    )(fine, ids, coarse)
+    return (fine.transpose(1, 0, 2), ids, coarse.transpose(1, 0, 2))
 
 
 def solution(mesh):

time: 21.8 us -> 21.2 us (0.972)
  local copies, waits for them, and re-layouts: 2.39 us -> 0 us
  Pallas kernels: 18 us -> 19.8 us
    unnamed x2 -> x0, local copies, waits for them, and re-layouts: 1.88 us -> none
    pallas_call x0 -> x1, Pallas kernels: none -> 1.83 us  [per_device(): pl.pallas_call(finish, out_shape=(jax.ShapeDtypeStruct(fine.shape, f32),...]
    squeeze x1 -> x0, local copies, waits for them, and re-layouts: 0.51 us -> none  [per_device(): ids[0, :capacity]]
where the time goes in v3:
time: 21.2 us; the launch traced here: 21 us
  Pallas kernels  19.8 us (93%)
  between operations  1.28 us (6%)
    pallas_call x1, Pallas kernels, per_device(): pl.pallas_call(functools.partial(kernel, group, levels, rounds), out_shap...  17.9 us
    pallas_call x1, Pallas kernels, per_device(): pl.pallas_call(finish, out_shape=(jax.ShapeDtypeStruct(fine.shape, f32),...  1.83 us

profile of v3, /device:TPU:0, one launch (start us, length us, event | category | flops | bytes accessed | tf_op | source)
XLA Modules:
  0.0 21.0 jit_solution(1793056338571657930)
XLA Ops:
  1.3 17.9 %shard_map.76 = (f32[5,20,4096]{2,1,0:T(8,128)S(1)}, s32[1,128]{1,0:T(1,128)S(1)}, f32[5,2,512]{2,1,0:T(2,128)S(1)}) custom-call(f32[5,20,4096]{2,1,0:T(8,128)} %bitcast.4, s32[20]{0:T(128)} %ids_ref.1, s32[1]{0:T(128)S(6)} %copy.8.live_ref, s32[2]{0:T(128)} %bitcast.5, s32[640]{0:T(1024)} %parent_ref.1), custom_call_target="tpu_custom_call" | custom-call | tf_op jit(solution)/shard_map/pallas_call | solution.py:324
  19.2 1.8 %shard_map.77 = (f32[5,20,4096]{2,1,0:T(8,128)}, s32[20]{0:T(128)}, f32[5,2,512]{2,1,0:T(2,128)}) custom-call(f32[5,20,4096]{2,1,0:T(8,128)S(1)} %get-tuple-element.9.fine_ref, s32[1,128]{1,0:T(1,128)S(1)} %get-tuple-element.10.marks_ref, f32[5,2,512]{2,1,0:T(2,128)S(1)} %get-tuple-element.11.sums_ref), custom_call_target="tpu_custom_call" | custom-call | tf_op jit(solution)/shard_map/pallas_call | solution.py:368

commit v4 on v3

--- a/solution.py
+++ b/solution.py
@@ -11,7 +11,8 @@
 SEND_MOST = 4
 PAR_DEV = 2
 LANES = 128
-AHEAD = 2
+AHEAD = 0
+SUMS_AT = 2
 ROWS = 8
 MESH = pl.DeviceIdType.MESH
 
@@ -39,7 +40,7 @@
     work, out_rows, in_rows, out_marks, in_marks,
     part, part_in, gathered, counts_ref, ids, parents_of,
     read_sem, small_sem, row_send, row_recv, mark_send, mark_recv,
-    a_send, a_recv, b_send, b_recv,
+    a_send, a_recv, b_send, b_recv, ready, go,
 ):
     variables, capacity, cells = x_ref.shape
     first_rows = -(-(capacity - SEND_MOST * rounds) // ROWS) * ROWS
@@ -65,10 +66,13 @@
         copy.start()
 
     barrier = pltpu.get_barrier_semaphore()
+    hub = group - 1
     for d in range(1, group):
-        pl.semaphore_signal(barrier, inc=1, device_id={"bal": lax.rem(bal + d, group)}, device_id_type=MESH)
-    for d in range(1, levels):
-        pl.semaphore_signal(barrier, inc=1, device_id={"level": lax.rem(level + d, levels)}, device_id_type=MESH)
+        to = lax.rem(bal + d, group)
+
+        @pl.when(to != hub)
+        def _(to=to):
+            pl.semaphore_signal(barrier, inc=1, device_id={"bal": to}, device_id_type=MESH)
 
     lane = lax.broadcasted_iota(jnp.int32, (ROWS, LANES), 1)
     small[0].wait()
@@ -140,6 +144,31 @@
             merged.append(jnp.where(slot < kept, tiles[t], fresh) if t < len(tiles) else fresh)
         return merged
 
+    def enter():
+        @pl.when(bal != hub)
+        def _():
+            pl.semaphore_wait(barrier, group - 1)
+            pl.semaphore_signal(ready, inc=1, device_id={"bal": hub}, device_id_type=MESH)
+
+        @pl.when(bal == hub)
+        def _():
+            pl.semaphore_wait(ready, group - 1)
+            for d in range(1, levels):
+                to = lax.rem(level + d, levels)
+                pl.semaphore_signal(barrier, inc=1, device_id={"level": to}, device_id_type=MESH)
+
+    def enter_levels():
+        @pl.when(bal == hub)
+        def _():
+            pl.semaphore_wait(barrier, levels - 1)
+            for d in range(1, group):
+                to = lax.rem(bal + d, group)
+                pl.semaphore_signal(go, inc=1, device_id={"bal": to}, device_id_type=MESH)
+
+        @pl.when(bal != hub)
+        def _():
+            pl.semaphore_wait(go, 1)
+
     sent = counts_ref[0]
     for v in range(variables):
         reads[v].wait()
@@ -155,7 +184,7 @@
 
         lax.fori_loop(0, chunks, body, 0)
         if v == 0:
-            pl.semaphore_wait(barrier, group - 1 + levels - 1)
+            enter()
         send_rows(0, v).start()
         if v == 0:
             for copy in small[1:]:
@@ -218,6 +247,9 @@
     def parent_sums():
         for v in range(variables):
             restrict_rows(v)
+
+    def send_sums():
+        enter_levels()
         for d in range(1, levels):
             send_a(d).start()
 
@@ -231,6 +263,8 @@
         for v in range(variables):
             if r == 1 and v == AHEAD:
                 parent_sums()
+            if r == 1 and v == SUMS_AT:
+                send_sums()
             send_rows(r - 1, v).wait_recv()
 
             def body(c, carry, v=v, r=r, kept=kept, count=count, held_count=held_count, sent=sent):
@@ -362,6 +396,8 @@
             dma((levels - 1,)),
             dma((group - 1,)),
             dma((group - 1,)),
+            pltpu.SemaphoreType.REGULAR,
+            pltpu.SemaphoreType.REGULAR,
         ],
         compiler_params=pltpu.CompilerParams(collective_id=0, has_side_effects=True, vmem_limit_bytes=24 << 20),
     )(hbm(patches.transpose(1, 0, 2)), hbm(patch_ids), live, hbm(counts.reshape(rounds)), hbm(parent_of))

time: 21.2 us -> 19.3 us (0.910)
  Pallas kernels: 19.8 us -> 17.9 us
    pallas_call x1, Pallas kernels: 17.9 us -> 16.1 us  [per_device(): pl.pallas_call(functools.partial(kernel, group, levels, rounds), out_shap...]
where the time goes in v4:
time: 19.3 us; the launch traced here: 19.2 us
  Pallas kernels  17.9 us (93%)
  between operations  1.28 us (7%)
    pallas_call x1, Pallas kernels, per_device(): pl.pallas_call(functools.partial(kernel, group, levels, rounds), out_shap...  16.1 us
    pallas_call x1, Pallas kernels, per_device(): pl.pallas_call(finish, out_shape=(jax.ShapeDtypeStruct(fine.shape, f32),...  1.83 us

profile of v4, /device:TPU:0, one launch (start us, length us, event | category | flops | bytes accessed | tf_op | source)
XLA Modules:
  0.0 19.2 jit_solution(11719241240540137494)
XLA Ops:
  1.3 16.1 %shard_map.76 = (f32[5,20,4096]{2,1,0:T(8,128)S(1)}, s32[1,128]{1,0:T(1,128)S(1)}, f32[5,2,512]{2,1,0:T(2,128)S(1)}) custom-call(f32[5,20,4096]{2,1,0:T(8,128)} %bitcast.4, s32[20]{0:T(128)} %ids_ref.1, s32[1]{0:T(128)S(6)} %copy.8.live_ref, s32[2]{0:T(128)} %bitcast.5, s32[640]{0:T(1024)} %parent_ref.1), custom_call_target="tpu_custom_call" | custom-call | tf_op jit(solution)/shard_map/pallas_call | solution.py:358
  17.4 1.8 %shard_map.77 = (f32[5,20,4096]{2,1,0:T(8,128)}, s32[20]{0:T(128)}, f32[5,2,512]{2,1,0:T(2,128)}) custom-call(f32[5,20,4096]{2,1,0:T(8,128)S(1)} %get-tuple-element.9.fine_ref, s32[1,128]{1,0:T(1,128)S(1)} %get-tuple-element.10.marks_ref, f32[5,2,512]{2,1,0:T(2,128)S(1)} %get-tuple-element.11.sums_ref), custom_call_target="tpu_custom_call" | custom-call | tf_op jit(solution)/shard_map/pallas_call | solution.py:404
